TPU v7x, 32 devices: a whole 2x2x4 slice. The times are simulated.
32 devices in a mesh: ctx: 4 (over z), head: 8 (over y, x, core).
Axes of the slice: x: 2, y: 2, z: 4, core: 2. Of those that a mesh axis runs over, the one named last changes fastest.
Arguments:
- inputs: bfloat16 [8, 64, 4096], P('head', None, 'ctx'), may hold values from -6 to 6
- dt: float32 [8, 4096], P('head', 'ctx'), may hold values from 0.03 to 0.3
- decay_rate: float32 [8], P('head'), may hold values from 0.0024414062 to 0.4, as said below
- skip: float32 [8], P('head'), may hold values from 0.5 to 1.5
- b_proj: bfloat16 [128, 4096], P(None, 'ctx'), may hold values from -1.1953125 to 1.1953125
- c_proj: bfloat16 [128, 4096], P(None, 'ctx'), may hold values from -1.1953125 to 1.1953125
- lengths: int32 [16], replicated, may hold values from 1 to 1024, 4096 in all
- grad_out: bfloat16 [8, 64, 4096], P('head', None, 'ctx'), may hold values from -0.59765625 to 0.59765625
Outputs:
- mixed: bfloat16 [8, 64, 4096], P('head', None, 'ctx')
- grad_inputs: bfloat16 [8, 64, 4096], P('head', None, 'ctx')
- grad_dt: float32 [8, 4096], P('head', 'ctx')
- grad_b: float32 [128, 4096], P('head', 'ctx')
- grad_c: float32 [128, 4096], P('head', 'ctx')
Inputs may be any that keep to these rules, and one draw needn't show every extreme that they name: `decay_rate`: each head's decay rate is positive.
All inputs are finite; a program needn't handle non-finite values.
Results may differ from a plain program's by a relative error of at most 0.001.
Values sent between devices are 32-bit elements; how exact they have to be, the bound alone decides.
A program may use at most 64 MiB of HBM per device.

v0:
```python
import jax
import jax.numpy as jnp
from jax import lax
from jax.sharding import PartitionSpec as P

BLOCK = 128


HIGH = lax.Precision.HIGHEST


def passed_along(block, axis, distance):
    devices = range(lax.axis_size(axis))
    route = [(i - distance, i) for i in devices if i - distance in devices]
    return lax.ppermute(block, axis, route)


def run_head(
    x_head,
    dt_head,
    b_vals,
    c_vals,
    segment,
    before_first,
    decay_rate,
    skip_gain,
    start_state,
    block_len,
):
    width_p = x_head.shape[0]
    width_n = b_vals.shape[0]
    block_count = x_head.shape[1] // block_len
    x_blocks = x_head.reshape(width_p, block_count, block_len).transpose(1, 0, 2)
    dt_blocks = dt_head.reshape(block_count, block_len)
    b_blocks = b_vals.reshape(width_n, block_count, block_len).transpose(1, 0, 2)
    c_blocks = c_vals.reshape(width_n, block_count, block_len).transpose(1, 0, 2)
    seg_blocks = segment.reshape(block_count, block_len)
    shifted = jnp.concatenate([before_first.reshape(1), segment[:-1]])
    prev_segs = shifted.reshape(block_count, block_len)[:, 0]
    lower_ones = (
        lax.broadcasted_iota(jnp.int32, (block_len, block_len), 0)
        >= lax.broadcasted_iota(jnp.int32, (block_len, block_len), 1)
    ).astype(jnp.float32)
    log_decay = -decay_rate * dt_blocks
    cumulative = jnp.dot(log_decay, lower_ones.T, precision=HIGH)
    pair_mask = (seg_blocks[:, :, None] == seg_blocks[:, None, :]) & (lower_ones[None] > 0)
    log_gap = jnp.where(pair_mask, cumulative[:, :, None] - cumulative[:, None, :], 0.0)
    decay_mat = jnp.where(pair_mask, jnp.exp(log_gap), 0.0)
    gram_mat = jnp.einsum("kni,knj->kij", c_blocks, b_blocks, precision=HIGH)
    scaled_in = x_blocks * dt_blocks[:, None, :]
    y_inner = jnp.einsum("kpj,kij->kpi", scaled_in, gram_mat * decay_mat, precision=HIGH)
    decay_in = jnp.where(seg_blocks == prev_segs[:, None], jnp.exp(cumulative), 0.0)
    last_seg = seg_blocks[:, -1]
    weight_out = jnp.where(
        seg_blocks == last_seg[:, None], jnp.exp(cumulative[:, -1:] - cumulative), 0.0
    )
    decay_all = jnp.where(last_seg == prev_segs, jnp.exp(cumulative[:, -1]), 0.0)
    local_end = jnp.einsum(
        "kpj,knj->kpn", scaled_in * weight_out[:, None, :], b_blocks, precision=HIGH
    )

    def advance(carry_state, block_data):
        decay_block, end_block = block_data
        return (decay_block * carry_state + end_block, carry_state)

    end_state, block_starts = lax.scan(advance, start_state, (decay_all, local_end))
    y_state = (
        jnp.einsum("kpn,kni->kpi", block_starts, c_blocks, precision=HIGH) * decay_in[:, None, :]
    )
    y_blocks = y_inner + y_state + skip_gain * x_blocks
    return (y_blocks.transpose(1, 0, 2).reshape(width_p, -1), end_state)


def per_device(inputs, dt, decay_rate, skip, b_proj, c_proj, lengths, grad_out):
    local_tok = inputs.shape[2]
    doc_ends = jnp.cumsum(lengths)
    my_index = lax.axis_index("ctx")
    ctx_count = lax.axis_size("ctx")
    offset = my_index * local_tok
    positions = offset + jnp.arange(local_tok, dtype=jnp.int32)
    segment = jnp.sum((positions[None, :] >= doc_ends[:-1, None]).astype(jnp.int32), axis=0)
    before_count = jnp.sum((offset - 1 >= doc_ends[:-1]).astype(jnp.int32))
    prev_dev = jnp.where(offset == 0, -1, before_count)
    x_float = inputs.astype(jnp.float32)
    grad_float = grad_out.astype(jnp.float32)
    b_float = b_proj.astype(jnp.float32)
    c_float = c_proj.astype(jnp.float32)
    lower_ones = (
        lax.broadcasted_iota(jnp.int32, (BLOCK, BLOCK), 0)
        >= lax.broadcasted_iota(jnp.int32, (BLOCK, BLOCK), 1)
    ).astype(jnp.float32)

    def summary(x_head, dt_head, rate_head, grad_head):
        log_blocks = (-rate_head * dt_head).reshape(-1, BLOCK)
        cum_blocks = jnp.dot(log_blocks, lower_ones.T, precision=HIGH)
        block_sums = cum_blocks[:, -1]
        prefix = jnp.cumsum(block_sums) - block_sums
        cum_device = (cum_blocks + prefix[:, None]).reshape(-1)
        total_log = cum_device[-1]
        decay_dev = jnp.where(segment[-1] == prev_dev, jnp.exp(total_log), 0.0)
        weight_out = jnp.where(segment == segment[-1], jnp.exp(total_log - cum_device), 0.0)
        state_dev = jnp.dot(x_head * (dt_head * weight_out)[None, :], b_float.T, precision=HIGH)
        weight_in = jnp.where(segment == prev_dev, jnp.exp(cum_device), 0.0)
        own_grad = jnp.dot(grad_head * weight_in[None, :], c_float.T, precision=HIGH)
        return (decay_dev, state_dev, own_grad)

    decay_dev, state_dev, own_grad = jax.vmap(summary)(x_float, dt, decay_rate, grad_float)
    empty_state = jnp.zeros_like(state_dev)

    def pass_state(turn, current):
        return passed_along(decay_dev[:, None, None] * current + state_dev, "ctx", 1)

    state_in = lax.fori_loop(0, ctx_count - 1, pass_state, empty_state)

    def pass_grad(turn, current):
        return passed_along(own_grad + decay_dev[:, None, None] * current, "ctx", -1)

    grad_next = lax.fori_loop(0, ctx_count - 1, pass_grad, empty_state)

    def forward(x_vals, dt_vals, b_vals, c_vals):

        def per_head(x_head, dt_head, rate_head, skip_head, start_state):
            return run_head(
                x_head,
                dt_head,
                b_vals,
                c_vals,
                segment,
                prev_dev,
                rate_head,
                skip_head,
                start_state,
                BLOCK,
            )

        return jax.vmap(per_head)(x_vals, dt_vals, decay_rate, skip, state_in)

    (mixed_float, end_state), pull_back = jax.vjp(forward, x_float, dt, b_float, c_float)
    grad_x, grad_step, grad_bv, grad_cv = pull_back((grad_float, grad_next))
    grad_b, grad_c = (
        lax.psum_scatter(grad_bv, "head", scatter_dimension=0, tiled=True),
        lax.psum_scatter(grad_cv, "head", scatter_dimension=0, tiled=True),
    )
    return (
        mixed_float.astype(jnp.bfloat16),
        grad_x.astype(jnp.bfloat16),
        grad_step,
        grad_b,
        grad_c,
    )


def solution(mesh):
    return jax.shard_map(
        per_device,
        mesh=mesh,
        in_specs=(
            P("head", None, "ctx"),
            P("head", "ctx"),
            P("head"),
            P("head"),
            P(None, "ctx"),
            P(None, "ctx"),
            P(),
            P("head", None, "ctx"),
        ),
        out_specs=(
            P("head", None, "ctx"),
            P("head", None, "ctx"),
            P("head", "ctx"),
            P("head", "ctx"),
            P("head", "ctx"),
        ),
        check_vma=False,
    )
```

profile of v0, /device:TPU:0, one launch (start us, length us, event | category | flops | bytes accessed | tf_op | source)
XLA Modules:
  0.0 176.9 jit_solution(5004268726711251436)
XLA Ops:
  19.9 18.2 %while.52 = (s32[]{:T(128)}, f32[1,64,128]{2,1,0:T(8,128)S(1)}, f32[1]{0:T(128)}, f32[1,64,128]{2,1,0:T(8,128)S(1)}, s32[]{:T(128)}) while((s32[]{:T(128)}, f32[1,64,128]{2,1,0:T(8,128)S(1)}, f32[1]{0:T(128)}, f32[1,64,128]{2,1,0:T(8,128)S(1)}, s32[]{:T(128)}) %tuple.106), condition=%wide.region_5.6_spmd, body=%wide.region_4.5_spmd.sunk | while | flops 16386 | bytes 229481 | solution.py:113
  19.9 4.9 %collective-permute-start = (f32[1,64,128]{2,1,0:T(8,128)S(1)}, f32[1,64,128]{2,1,0:T(8,128)S(1)}, u32[]{:S(2)}, u32[]{:S(2)}) collective-permute-start(f32[1,64,128]{2,1,0:T(8,128)S(1)} %multiply_add_fusion.4), channel_id=1, source_target_pairs={{0,8},{8,16},{16,24},{1,9},{9,17},{17,25},{2,10},{10,18},{18,26},{... | collective-permute-start | bytes 98312 | tf_op jit(solution)/shard_map/while/body/eval_jaxpr/ppermute | solution.py:15
  24.9 1.6 collective-permute-done
  26.4 4.2 %collective-permute-start = (f32[1,64,128]{2,1,0:T(8,128)S(1)}, f32[1,64,128]{2,1,0:T(8,128)S(1)}, u32[]{:S(2)}, u32[]{:S(2)}) collective-permute-start(f32[1,64,128]{2,1,0:T(8,128)S(1)} %multiply_add_fusion.4), channel_id=1, source_target_pairs={{0,8},{8,16},{16,24},{1,9},{9,17},{17,25},{2,10},{10,18},{18,26},{... | collective-permute-start | bytes 98312 | tf_op jit(solution)/shard_map/while/body/eval_jaxpr/ppermute | solution.py:15
  30.7 1.6 collective-permute-done
  32.3 4.2 %collective-permute-start = (f32[1,64,128]{2,1,0:T(8,128)S(1)}, f32[1,64,128]{2,1,0:T(8,128)S(1)}, u32[]{:S(2)}, u32[]{:S(2)}) collective-permute-start(f32[1,64,128]{2,1,0:T(8,128)S(1)} %multiply_add_fusion.4), channel_id=1, source_target_pairs={{0,8},{8,16},{16,24},{1,9},{9,17},{17,25},{2,10},{10,18},{18,26},{... | collective-permute-start | bytes 98312 | tf_op jit(solution)/shard_map/while/body/eval_jaxpr/ppermute | solution.py:15
  36.5 1.6 collective-permute-done
  38.1 15.5 %while.53 = (s32[]{:T(128)}, f32[1,64,128]{2,1,0:T(8,128)S(1)}, f32[8,1,64,128]{3,2,1,0:T(8,128)S(1)}, f32[8,1,1,1]{0,3,2,1:T(1,128)S(1)}, f32[8,1]{1,0:T(8,128)...) while((s32[]{:T(128)}, f32[1,64,128]{2,1,0:T(8,128)S(1)}, f32[8,1,64,128]{3,2,1,0:T(8,128)S(1)}, ...), condition=%wide.region_7.8_spmd, body=%wide.region_6.7_spmd.sunk | while | flops 16386 | bytes 163961 | solution.py:66
  53.6 0.9 copy-done.1
  55.6 18.0 %while.54 = (s32[]{:T(128)}, f32[1,64,128]{2,1,0:T(8,128)S(1)}, f32[1]{0:T(128)}, f32[1,64,128]{2,1,0:T(8,128)S(1)}, s32[]{:T(128)}) while((s32[]{:T(128)}, f32[1,64,128]{2,1,0:T(8,128)S(1)}, f32[1]{0:T(128)}, f32[1,64,128]{2,1,0:T(8,128)S(1)}, s32[]{:T(128)}) %tuple.112), condition=%wide.region_9.10_spmd, body=%wide.region_8.9_spmd.sunk | while | flops 16386 | bytes 229481 | solution.py:118
  55.6 1.3 collective-permute-start.1
  56.9 4.8 %collective-permute-done.1 = f32[1,64,128]{2,1,0:T(8,128)S(1)} collective-permute-done((f32[1,64,128]{2,1,0:T(8,128)S(1)}, f32[1,64,128]{2,1,0:T(8,128)S(1)}, u32[]{:S(2)}, u32[]{:S(2)}) %collective-permute-start.1) | collective-permute-done | bytes 32800 | tf_op jit(solution)/shard_map/while/body/eval_jaxpr/ppermute | solution.py:15
  61.7 1.3 collective-permute-start.1
  63.0 4.8 %collective-permute-done.1 = f32[1,64,128]{2,1,0:T(8,128)S(1)} collective-permute-done((f32[1,64,128]{2,1,0:T(8,128)S(1)}, f32[1,64,128]{2,1,0:T(8,128)S(1)}, u32[]{:S(2)}, u32[]{:S(2)}) %collective-permute-start.1) | collective-permute-done | bytes 32800 | tf_op jit(solution)/shard_map/while/body/eval_jaxpr/ppermute | solution.py:15
  67.8 1.3 collective-permute-start.1
  69.1 4.5 %collective-permute-done.1 = f32[1,64,128]{2,1,0:T(8,128)S(1)} collective-permute-done((f32[1,64,128]{2,1,0:T(8,128)S(1)}, f32[1,64,128]{2,1,0:T(8,128)S(1)}, u32[]{:S(2)}, u32[]{:S(2)}) %collective-permute-start.1) | collective-permute-done | bytes 32800 | tf_op jit(solution)/shard_map/while/body/eval_jaxpr/ppermute | solution.py:15
  73.6 20.5 %while.55 = (s32[]{:T(128)}, f32[1,64,128]{2,1,0:T(8,128)S(1)}, f32[8,1]{1,0:T(8,128)S(1)}, f32[8,1,64,128]{3,2,1,0:T(8,128)S(1)}, f32[8,1,64,128]{3,2,1,0:T(8,1...) while((s32[]{:T(128)}, f32[1,64,128]{2,1,0:T(8,128)S(1)}, ...), condition=%wide.region_12.13_spmd, body=%wide.region_10.12_spmd.sunk | while | flops 32770 | bytes 196761 | solution.py:66
  74.2 1.3 fusion.132
  76.8 1.3 fusion.132
  79.3 1.3 fusion.132
  81.9 1.3 fusion.132
  84.5 1.3 fusion.132
  87.0 1.3 fusion.132
  89.6 1.3 fusion.132
  92.1 1.3 fusion.132
  95.0 1.0 fusion.1
  96.0 1.0 copy.67
  97.9 1.0 fusion.2
  98.9 1.0 copy.68
  103.6 1.3 fusion.7
  106.5 25.5 %reduce-scatter.3.cloned.1.call-done = f32[16,1024]{1,0:T(8,128)} async-done(((f32[128,1024]{1,0:T(8,128)}), f32[16,1024]{1,0:T(8,128)}) %reduce-scatter.3.cloned.1.call-update) | async-done | bytes 65552 | tf_op jit(solution)/shard_map/reduce_scatter | solution.py:141
  132.0 38.1 %reduce-scatter.5.cloned.1.call-done = f32[16,1024]{1,0:T(8,128)} async-done(((f32[128,1024]{1,0:T(8,128)}), f32[16,1024]{1,0:T(8,128)}) %reduce-scatter.5.cloned.1.call-update) | async-done | bytes 65552 | tf_op jit(solution)/shard_map/reduce_scatter | solution.py:142
  (126 shorter events, 43.0 us)
Async XLA Ops:
  7.2 11.6 %copy-start = (bf16[128,1024]{1,0:T(8,128)(2,1)S(1)}, bf16[128,1024]{1,0:T(8,128)(2,1)}, u32[]{:S(2)}) copy-start(bf16[128,1024]{1,0:T(8,128)(2,1)} %param.20) | copy-start | bytes 786436
  7.2 8.9 %copy-start.3 = (bf16[1,64,1024]{2,1,0:T(8,128)(2,1)S(1)}, bf16[1,64,1024]{2,1,0:T(8,128)(2,1)}, u32[]{:S(2)}) copy-start(bf16[1,64,1024]{2,1,0:T(8,128)(2,1)} %param.16) | copy-start | bytes 393220
  7.2 124.8 %reduce-scatter.3.cloned.1.call-start = ((), (), s32[]{:S(2)}) async-start(), calls=%async_computation.2 | async-start | bytes 589824 | tf_op jit(solution)/shard_map/reduce_scatter | solution.py:141
  16.1 0.9 copy-start.2
  17.0 0.7 copy-start.4
  19.9 6.5 %collective-permute-start = (f32[1,64,128]{2,1,0:T(8,128)S(1)}, f32[1,64,128]{2,1,0:T(8,128)S(1)}, u32[]{:S(2)}, u32[]{:S(2)}) collective-permute-start(f32[1,64,128]{2,1,0:T(8,128)S(1)} %multiply_add_fusion.4), channel_id=1, source_target_pairs={{0,8},{8,16},{16,24},{1,9},{9,17},{17,25},{2,10},{10,18},{18,26},{... | collective-permute-start | bytes 98312 | tf_op jit(solution)/shard_map/while/body/eval_jaxpr/ppermute | solution.py:15
  26.4 5.8 %collective-permute-start = (f32[1,64,128]{2,1,0:T(8,128)S(1)}, f32[1,64,128]{2,1,0:T(8,128)S(1)}, u32[]{:S(2)}, u32[]{:S(2)}) collective-permute-start(f32[1,64,128]{2,1,0:T(8,128)S(1)} %multiply_add_fusion.4), channel_id=1, source_target_pairs={{0,8},{8,16},{16,24},{1,9},{9,17},{17,25},{2,10},{10,18},{18,26},{... | collective-permute-start | bytes 98312 | tf_op jit(solution)/shard_map/while/body/eval_jaxpr/ppermute | solution.py:15
  32.3 5.8 %collective-permute-start = (f32[1,64,128]{2,1,0:T(8,128)S(1)}, f32[1,64,128]{2,1,0:T(8,128)S(1)}, u32[]{:S(2)}, u32[]{:S(2)}) collective-permute-start(f32[1,64,128]{2,1,0:T(8,128)S(1)} %multiply_add_fusion.4), channel_id=1, source_target_pairs={{0,8},{8,16},{16,24},{1,9},{9,17},{17,25},{2,10},{10,18},{18,26},{... | collective-permute-start | bytes 98312 | tf_op jit(solution)/shard_map/while/body/eval_jaxpr/ppermute | solution.py:15
  53.6 1.0 copy-start.1
  55.6 6.1 %collective-permute-start.1 = (f32[1,64,128]{2,1,0:T(8,128)S(1)}, f32[1,64,128]{2,1,0:T(8,128)S(1)}, u32[]{:S(2)}, u32[]{:S(2)}) collective-permute-start(f32[1,64,128]{2,1,0:T(8,128)S(1)} %multiply_add_fusion.5), channel_id=1, source_target_pairs={{8,0},{16,8},{24,16},{9,1},{17,9},{25,17},{10,2},{18,10},{26,18},{... | collective-permute-start | bytes 98312 | tf_op jit(solution)/shard_map/while/body/eval_jaxpr/ppermute | solution.py:15
  61.7 6.1 %collective-permute-start.1 = (f32[1,64,128]{2,1,0:T(8,128)S(1)}, f32[1,64,128]{2,1,0:T(8,128)S(1)}, u32[]{:S(2)}, u32[]{:S(2)}) collective-permute-start(f32[1,64,128]{2,1,0:T(8,128)S(1)} %multiply_add_fusion.5), channel_id=1, source_target_pairs={{8,0},{16,8},{24,16},{9,1},{17,9},{25,17},{10,2},{18,10},{26,18},{... | collective-permute-start | bytes 98312 | tf_op jit(solution)/shard_map/while/body/eval_jaxpr/ppermute | solution.py:15
  67.8 5.8 %collective-permute-start.1 = (f32[1,64,128]{2,1,0:T(8,128)S(1)}, f32[1,64,128]{2,1,0:T(8,128)S(1)}, u32[]{:S(2)}, u32[]{:S(2)}) collective-permute-start(f32[1,64,128]{2,1,0:T(8,128)S(1)} %multiply_add_fusion.5), channel_id=1, source_target_pairs={{8,0},{16,8},{24,16},{9,1},{17,9},{25,17},{10,2},{18,10},{26,18},{... | collective-permute-start | bytes 98312 | tf_op jit(solution)/shard_map/while/body/eval_jaxpr/ppermute | solution.py:15
  97.0 73.1 %reduce-scatter.5.cloned.1.call-start = ((), (), s32[]{:S(2)}) async-start(), calls=%async_computation.3 | async-start | bytes 589824 | tf_op jit(solution)/shard_map/reduce_scatter | solution.py:142
Sparse Core Ops, SparseCore 0:
  97.1 34.7 reduce-scatter.2
  135.9 34.1 reduce-scatter.4
where the time goes:
time: 178 us; the launch traced here: 177 us
  waiting for transfers between devices  82.5 us (46%)
  local copies, waits for them, and re-layouts  29 us (16%)
  other arithmetic  19 us (11%)
  between operations  17.6 us (10%)
  starting transfers between devices  17.3 us (10%)
  matrix products  11.2 us (6%)
    reduce_scatter x1, waiting for transfers between devices, per_device(): lax.psum_scatter(grad_cv, 'head', scatter_dimension=0, tiled=True)  38.1 us
    reduce_scatter x1, waiting for transfers between devices, per_device(): lax.psum_scatter(grad_bv, 'head', scatter_dimension=0, tiled=True)  25.5 us
    ppermute x6, waiting for transfers between devices, passed_along(): return lax.ppermute(block, axis, route)  18.8 us
    ppermute x6, starting transfers between devices, passed_along(): return lax.ppermute(block, axis, route)  17.2 us
    dynamic_update_slice x32, local copies, waits for them, and re-layouts, run_head(): lax.scan(advance, start_state, (decay_all, local_end))  11.5 us
    reduce_sum x8, other arithmetic, advance(): return (decay_block * carry_state + end_block, carry_state)  10.1 us
    dynamic_slice x16, local copies, waits for them, and re-layouts, run_head(): lax.scan(advance, start_state, (decay_all, local_end))  8.86 us
    add x8, other arithmetic, advance(): return (decay_block * carry_state + end_block, carry_state)  5.23 us
  transfers between devices with their start and end apart: 8, of which 8 were waited for; matrix products, arithmetic and copies ran while one was open for 5% of the time, Pallas kernels for 0%

commit v1 on v0

v1 whole, which is shorter than its diff:
```python
import functools
import jax
import jax.numpy as jnp
from jax import lax
from jax.experimental import pallas as pl
from jax.experimental.pallas import tpu as pltpu
from jax.sharding import PartitionSpec as P

Q = 128
HIGH = lax.Precision.HIGHEST
F32 = jnp.float32
BF16 = jnp.bfloat16
MESH = pl.DeviceIdType.MESH


def mm(a, b, ca, cb):
    return lax.dot_general(a, b, (((ca,), (cb,)), ((), ())), preferred_element_type=F32)


def split(v):
    hi = v.astype(BF16)
    return hi, (v - hi.astype(F32)).astype(BF16)


def lanes(a, b):
    return jnp.concatenate([a, b], axis=1)


def rows(a, b):
    return jnp.concatenate([a, b], axis=0)


def kernel(cfg, rate_ref, skip_ref, len_ref, x_ref, dt_ref, b_ref, c_ref, g_ref, *refs):
    n_ctx, n_head, hops, fused, ndoc = cfg
    mixed_ref, gx_ref, gdt_ref, gb_ref, gc_ref = refs[:5]
    (s_ref, gz_ref, y_ref, v_ref, out_s, out_g, in_s, in_g, ctx_send, ctx_recv) = refs[5:15]
    if fused:
        part, recv1, send2, recv2, s1_send, s1_recv, s2_send, s2_recv = refs[15:]
    width_p = x_ref.shape[1]
    local = x_ref.shape[2]
    width_n = b_ref.shape[0]
    blocks = local // Q
    me = lax.axis_index("ctx")
    head = lax.axis_index("head")
    chips = n_head // 2
    core = lax.rem(head, 2)
    chip = head // 2

    barrier = pltpu.get_barrier_semaphore()

    @pl.when(me > 0)
    def _():
        pl.semaphore_signal(barrier, inc=1, device_id={"ctx": me - 1}, device_id_type=MESH)

    @pl.when(me < n_ctx - 1)
    def _():
        pl.semaphore_signal(barrier, inc=1, device_id={"ctx": me + 1}, device_id_type=MESH)

    if fused:
        pl.semaphore_signal(
            barrier, inc=1, device_id={"head": chip * 2 + 1 - core}, device_id_type=MESH
        )
        for d in range(1, chips):
            to = lax.rem(chip + d, chips) * 2 + core
            pl.semaphore_signal(barrier, inc=1, device_id={"head": to}, device_id_type=MESH)

    rate = rate_ref[0]
    skip = skip_ref[0]
    offset = me * local

    ends = []
    total = len_ref[0]
    for j in range(ndoc - 1):
        ends.append(total)
        total = total + len_ref[j + 1]

    def segment_of(pos):
        seg = jnp.zeros(pos.shape, jnp.int32)
        for end in ends:
            seg = seg + (pos >= end).astype(jnp.int32)
        return seg

    pos8 = (
        offset
        + lax.broadcasted_iota(jnp.int32, (blocks, Q), 0) * Q
        + lax.broadcasted_iota(jnp.int32, (blocks, Q), 1)
    )
    pos_t = (
        offset
        + lax.broadcasted_iota(jnp.int32, (Q, blocks), 1) * Q
        + lax.broadcasted_iota(jnp.int32, (Q, blocks), 0)
    )
    seg8 = segment_of(pos8)
    seg_t = segment_of(pos_t)
    before8 = jnp.where(pos8 == 0, -1, segment_of(pos8 - 1))
    prev8 = before8[:, 0:1]
    last8 = seg8[:, Q - 1 : Q]

    dt8 = jnp.concatenate([dt_ref[0:1, k * Q : (k + 1) * Q] for k in range(blocks)], axis=0)
    row_i = lax.broadcasted_iota(jnp.int32, (Q, Q), 0)
    col_j = lax.broadcasted_iota(jnp.int32, (Q, Q), 1)
    lower = row_i >= col_j
    lower_ones = lower.astype(F32)
    log8 = -rate * dt8
    cum8 = lax.dot_general(
        log8, lower_ones, (((1,), (1,)), ((), ())), precision=HIGH, preferred_element_type=F32
    )
    cum_t = lax.dot_general(
        lower_ones, log8, (((1,), (1,)), ((), ())), precision=HIGH, preferred_element_type=F32
    )
    end8 = cum8[:, Q - 1 : Q]
    din8 = jnp.where(seg8 == prev8, jnp.exp(cum8), 0.0)
    wdt8 = jnp.where(seg8 == last8, jnp.exp(end8 - cum8), 0.0) * dt8
    dall8 = jnp.where(last8 == prev8, jnp.exp(end8), 0.0)

    def cut(ref, k):
        return ref[0, :, k * Q : (k + 1) * Q]

    def cut2(ref, k):
        return ref[:, k * Q : (k + 1) * Q]

    state = jnp.zeros((width_p, width_n), F32)
    for k in range(blocks):
        s_ref[k] = state
        b_k = cut2(b_ref, k)
        hi, lo = split(cut(x_ref, k).astype(F32) * wdt8[k : k + 1])
        state = dall8[k : k + 1] * state + mm(lanes(hi, lo), lanes(b_k, b_k), 1, 1)
    out_s[0] = state
    carry = jnp.zeros((width_p, width_n), F32)
    for k in reversed(range(blocks)):
        gz_ref[k] = carry
        c_k = cut2(c_ref, k)
        hi, lo = split(cut(g_ref, k).astype(F32) * din8[k : k + 1])
        carry = dall8[k : k + 1] * carry + mm(lanes(hi, lo), lanes(c_k, c_k), 1, 1)
    out_g[0] = carry

    ahead = [None] * blocks
    prod = jnp.ones((1, 1), F32)
    for k in range(blocks):
        ahead[k] = prod
        prod = prod * dall8[k : k + 1]
    decay_dev = prod
    behind = [None] * blocks
    prod = jnp.ones((1, 1), F32)
    for k in reversed(range(blocks)):
        behind[k] = prod
        prod = prod * dall8[k : k + 1]

    @pl.when(me == 0)
    def _():
        in_s[...] = jnp.zeros_like(in_s)

    @pl.when(me == n_ctx - 1)
    def _():
        in_g[...] = jnp.zeros_like(in_g)

    peers = chips if fused else 0
    at_end = (me == 0) | (me == n_ctx - 1)

    @pl.when(at_end)
    def _():
        pl.semaphore_wait(barrier, peers + 1)

    @pl.when(jnp.logical_not(at_end))
    def _():
        pl.semaphore_wait(barrier, peers + 2)

    def ctx_copy(r, way):
        src, dst = (out_s, in_s) if way == 0 else (out_g, in_g)
        return pltpu.make_async_remote_copy(
            src_ref=src.at[r],
            dst_ref=dst.at[r],
            send_sem=ctx_send.at[r, way],
            recv_sem=ctx_recv.at[r, way],
            device_id={"ctx": me + 1 if way == 0 else me - 1},
            device_id_type=MESH,
        )

    def ctx_start(r):
        @pl.when(me < n_ctx - 1)
        def _():
            ctx_copy(r, 0).start()

        @pl.when(me > 0)
        def _():
            ctx_copy(r, 1).start()

    def ctx_wait(r):
        @pl.when(me > 0)
        def _():
            ctx_copy(r, 0).wait_recv()

        @pl.when(me < n_ctx - 1)
        def _():
            ctx_copy(r, 1).wait_recv()

    def ctx_done(r):
        @pl.when(me < n_ctx - 1)
        def _():
            ctx_copy(r, 0).wait_send()

        @pl.when(me > 0)
        def _():
            ctx_copy(r, 1).wait_send()

    ctx_start(0)

    def put(k, way, value, add):
        if fused:
            each = width_n // n_head
            chunk, lo = k // 2, (k % 2) * Q
            for h in range(n_head):
                at = (chunk, h % 2, h // 2, slice(way * each, (way + 1) * each), slice(lo, lo + Q))
                piece = value[h * each : (h + 1) * each]
                part[at] = part[at] + piece if add else piece
        else:
            ref = (gb_ref, gc_ref)[way]
            at = (slice(None), slice(k * Q, (k + 1) * Q))
            ref[at] = ref[at] + value if add else value

    def intra(k):
        x_k, g_k, b_k, c_k = cut(x_ref, k), cut(g_ref, k), cut2(b_ref, k), cut2(c_ref, k)
        mask = lower & (seg_t[:, k : k + 1] == seg8[k : k + 1])
        gap = jnp.where(mask, cum_t[:, k : k + 1] - cum8[k : k + 1], 0.0)
        ddt = jnp.where(mask, jnp.exp(gap), 0.0) * dt8[k : k + 1]
        a_hi, a_lo = split(mm(c_k, b_k, 0, 0) * ddt)
        w_hi, w_lo = split(mm(g_k, x_k, 0, 0) * ddt)
        y_ref[:, k * Q : (k + 1) * Q] = mm(lanes(x_k, x_k), lanes(a_hi, a_lo), 1, 1)
        v_ref[:, k * Q : (k + 1) * Q] = mm(lanes(g_k, g_k), rows(a_hi, a_lo), 1, 0)
        put(k, 0, mm(lanes(c_k, c_k), rows(w_hi, w_lo), 1, 0), False)
        put(k, 1, mm(lanes(b_k, b_k), lanes(w_hi, w_lo), 1, 1), False)

    diffs, qs, tails = [None] * blocks, [None] * blocks, [None] * blocks

    def start_state(k, state_in):
        return s_ref[k] + ahead[k] * state_in

    def inter(k, state_in, grad_in):
        x_k, g_k, b_k, c_k = cut(x_ref, k), cut(g_ref, k), cut2(b_ref, k), cut2(c_ref, k)
        s_k = start_state(k, state_in)
        gz = gz_ref[k] + behind[k] * grad_in
        if k + 1 < blocks:
            s_end = start_state(k + 1, state_in)
        else:
            s_end = out_s[0] + decay_dev * state_in
        tails[k] = jnp.sum(jnp.sum(gz * s_end, axis=0, keepdims=True), axis=1, keepdims=True)
        s_hi, s_lo = split(s_k)
        z_hi, z_lo = split(gz)
        din, wdt = din8[k : k + 1], wdt8[k : k + 1]
        at = (slice(None), slice(k * Q, (k + 1) * Q))
        y = y_ref[at] + mm(lanes(s_hi, s_lo), rows(c_k, c_k), 1, 0) * din
        v = v_ref[at] + mm(lanes(z_hi, z_lo), rows(b_k, b_k), 1, 0) * wdt
        x_f, g_f = x_k.astype(F32), g_k.astype(F32)
        mixed_ref[0, :, k * Q : (k + 1) * Q] = (y + skip * x_f).astype(BF16)
        gx_ref[0, :, k * Q : (k + 1) * Q] = (v + skip * g_f).astype(BF16)
        q_k = jnp.sum(x_f * v, axis=0, keepdims=True)
        qs[k] = q_k
        diffs[k] = jnp.sum(g_f * y, axis=0, keepdims=True) - q_k
        put(k, 0, mm(rows(z_hi, z_lo), rows(x_k, x_k), 0, 0) * wdt, True)
        put(k, 1, mm(rows(s_hi, s_lo), rows(g_k, g_k), 0, 0) * din, True)

    def pair_copy(chunk):
        return pltpu.make_async_remote_copy(
            src_ref=part.at[chunk, 1 - core],
            dst_ref=recv1.at[chunk],
            send_sem=s1_send.at[chunk],
            recv_sem=s1_recv.at[chunk],
            device_id={"head": chip * 2 + 1 - core},
            device_id_type=MESH,
        )

    def chip_copy(chunk, d):
        to = lax.rem(chip + d, chips)
        return pltpu.make_async_remote_copy(
            src_ref=send2.at[chunk, to],
            dst_ref=recv2.at[chunk, d - 1],
            send_sem=s2_send.at[chunk, d - 1],
            recv_sem=s2_recv.at[chunk, d - 1],
            device_id={"head": to * 2 + core},
            device_id_type=MESH,
        )

    def second(chunk):
        pair_copy(chunk).wait_recv()
        send2[chunk] = part[chunk, core] + recv1[chunk]
        for d in range(1, chips):
            chip_copy(chunk, d).start()

    early = blocks // 2
    for k in range(early):
        intra(k)
    ctx_wait(0)
    for r in range(1, hops):
        out_s[r] = out_s[0] + decay_dev * in_s[r - 1]
        out_g[r] = out_g[0] + decay_dev * in_g[r - 1]
        ctx_start(r)
        ctx_wait(r)
    state_in = in_s[hops - 1]
    grad_in = in_g[hops - 1]
    for k in range(blocks):
        if k >= early:
            intra(k)
        inter(k, state_in, grad_in)
        if fused and k % 2 == 1:
            chunk = k // 2
            pair_copy(chunk).start()
            if chunk > 0:
                second(chunk - 1)

    q8 = jnp.concatenate(qs, axis=0)
    r8 = jnp.concatenate(diffs, axis=0)
    tail8 = jnp.concatenate(tails, axis=0)
    back8 = lax.dot_general(
        r8, lower_ones, (((1,), (0,)), ((), ())), precision=HIGH, preferred_element_type=F32
    )
    gdt8 = q8 / dt8 - rate * (back8 + tail8)
    for k in range(blocks):
        gdt_ref[0:1, k * Q : (k + 1) * Q] = gdt8[k : k + 1]

    for r in range(hops):
        ctx_done(r)
    if fused:
        each = width_n // n_head
        chunks = blocks // 2
        second(chunks - 1)
        for chunk in range(chunks):
            total = send2[chunk, chip]
            for d in range(1, chips):
                chip_copy(chunk, d).wait_recv()
                total = total + recv2[chunk, d - 1]
            at = slice(chunk * 2 * Q, (chunk + 1) * 2 * Q)
            gb_ref[:, at] = total[:each]
            gc_ref[:, at] = total[each:]
        for chunk in range(chunks):
            pair_copy(chunk).wait_send()
            for d in range(1, chips):
                chip_copy(chunk, d).wait_send()


def per_device(n_ctx, n_head, inputs, dt, decay_rate, skip, b_proj, c_proj, lengths, grad_out):
    _, width_p, local = inputs.shape
    width_n = b_proj.shape[0]
    longest = n_ctx * local // 4
    hops = max(1, min(n_ctx - 1, (longest - 2) // local + 1))
    each = width_n // n_head
    fused = each % 8 == 0
    blocks = local // Q
    chips = n_head // 2
    chunks = blocks // 2
    vmem = pl.BlockSpec(memory_space=pltpu.VMEM)
    smem = pl.BlockSpec(memory_space=pltpu.SMEM)
    grad_rows = each if fused else width_n
    scratch = [
        pltpu.VMEM((blocks, width_p, width_n), F32),
        pltpu.VMEM((blocks, width_p, width_n), F32),
        pltpu.VMEM((width_p, local), F32),
        pltpu.VMEM((width_p, local), F32),
        pltpu.VMEM((hops, width_p, width_n), F32),
        pltpu.VMEM((hops, width_p, width_n), F32),
        pltpu.VMEM((hops, width_p, width_n), F32),
        pltpu.VMEM((hops, width_p, width_n), F32),
        pltpu.SemaphoreType.DMA((hops, 2)),
        pltpu.SemaphoreType.DMA((hops, 2)),
    ]
    if fused:
        scratch += [
            pltpu.VMEM((chunks, 2, chips, 2 * each, 2 * Q), F32),
            pltpu.VMEM((chunks, chips, 2 * each, 2 * Q), F32),
            pltpu.VMEM((chunks, chips, 2 * each, 2 * Q), F32),
            pltpu.VMEM((chunks, chips - 1, 2 * each, 2 * Q), F32),
            pltpu.SemaphoreType.DMA((chunks,)),
            pltpu.SemaphoreType.DMA((chunks,)),
            pltpu.SemaphoreType.DMA((chunks, chips - 1)),
            pltpu.SemaphoreType.DMA((chunks, chips - 1)),
        ]
    mixed, gx, gdt, gb, gc = pl.pallas_call(
        functools.partial(kernel, (n_ctx, n_head, hops, fused, lengths.shape[0])),
        out_shape=(
            jax.ShapeDtypeStruct(inputs.shape, BF16),
            jax.ShapeDtypeStruct(inputs.shape, BF16),
            jax.ShapeDtypeStruct(dt.shape, F32),
            jax.ShapeDtypeStruct((grad_rows, local), F32),
            jax.ShapeDtypeStruct((grad_rows, local), F32),
        ),
        in_specs=[smem, smem, smem, vmem, vmem, vmem, vmem, vmem],
        out_specs=(vmem,) * 5,
        scratch_shapes=scratch,
        compiler_params=pltpu.CompilerParams(collective_id=0, has_side_effects=True),
    )(decay_rate, skip, lengths, inputs, dt, b_proj, c_proj, grad_out)
    if not fused:
        gb = lax.psum_scatter(gb, "head", scatter_dimension=0, tiled=True)
        gc = lax.psum_scatter(gc, "head", scatter_dimension=0, tiled=True)
    return mixed, gx, gdt, gb, gc


def solution(mesh):
    return jax.shard_map(
        functools.partial(per_device, mesh.shape["ctx"], mesh.shape["head"]),
        mesh=mesh,
        in_specs=(
            P("head", None, "ctx"),
            P("head", "ctx"),
            P("head"),
            P("head"),
            P(None, "ctx"),
            P(None, "ctx"),
            P(),
            P("head", None, "ctx"),
        ),
        out_specs=(
            P("head", None, "ctx"),
            P("head", None, "ctx"),
            P("head", "ctx"),
            P("head", "ctx"),
            P("head", "ctx"),
        ),
        check_vma=False,
    )
```

time: 178 us -> 24.8 us (0.14)
  waiting for transfers between devices: 82.5 us -> 0 us
  local copies, waits for them, and re-layouts: 29 us -> 4.37 us
  other arithmetic: 19 us -> 0 us
  Pallas kernels: 0 us -> 18.2 us
  starting transfers between devices: 17.3 us -> 0 us
  between operations: 17.6 us -> 1.95 us
  matrix products: 11.2 us -> 0 us
    reduce_scatter x2 -> x0, waiting for transfers between devices: 63.6 us -> none  [the longest x1 38.1 us: per_device(): lax.psum_scatter(grad_cv, 'head', scatter_dimension=0, tiled=True)]
    ppermute x6 -> x0, waiting for transfers between devices: 18.8 us -> none  [passed_along(): return lax.ppermute(block, axis, route)]
    pallas_call x0 -> x1, Pallas kernels: none -> 18.2 us  [per_device(): pl.pallas_call(functools.partial(kernel, (n_ctx, n_head, hops, fused, len...]
    ppermute x6 -> x0, starting transfers between devices: 17.2 us -> none  [passed_along(): return lax.ppermute(block, axis, route)]
    dynamic_update_slice x32 -> x0, local copies, waits for them, and re-layouts: 11.5 us -> none  [run_head(): lax.scan(advance, start_state, (decay_all, local_end))]
    dot_general x17 -> x0, matrix products: 11.2 us -> none  [the longest x3 2.42 us: run_head(): jnp.einsum('kpj,kij->kpi', scaled_in, gram_mat * decay_mat, precision=HIGH)]
    reduce_sum x11 -> x0, other arithmetic: 11 us -> none  [the longest x8 10.1 us: advance(): return (decay_block * carry_state + end_block, carry_state)]
    dynamic_slice x16 -> x0, local copies, waits for them, and re-layouts: 8.86 us -> none  [run_head(): lax.scan(advance, start_state, (decay_all, local_end))]
  transfers between devices with their start and end apart: 8 -> 0, of which waited for: 8 -> 0; matrix products, arithmetic and copies ran while one was open for 5% -> 0% of each run, Pallas kernels for 0% -> 0%
where the time goes in v1:
time: 24.8 us; the launch traced here: 24.6 us
  Pallas kernels  18.2 us (73%)
  local copies, waits for them, and re-layouts  4.37 us (18%)
  between operations  1.95 us (8%)
    pallas_call x1, Pallas kernels, per_device(): pl.pallas_call(functools.partial(kernel, (n_ctx, n_head, hops, fused, len...  18.2 us
    unnamed x13, local copies, waits for them, and re-layouts  4.37 us

profile of v1, /device:TPU:0, one launch (start us, length us, event | category | flops | bytes accessed | tf_op | source)
XLA Modules:
  0.0 24.6 jit_solution(5797934789915918331)
XLA Ops:
  1.9 18.2 %shard_map.119 = (bf16[1,64,1024]{2,1,0:T(8,128)(2,1)}, bf16[1,64,1024]{2,1,0:T(8,128)(2,1)}, f32[1,1024]{1,0:T(1,128)}, f32[16,1024]{1,0:T(8,128)}, f32[16,1024]{1,0:T(8,128)}) custom-call(f32[1]{0:T(128)S(6)} %copy.18.rate_ref, f32[1]{0:T(128)S(6)} %copy.19.skip_ref, s32[16]{0:T(128)} %len_ref.1, bf16[1,64,1024]{2,1,0:T(8,128)(2,1)} %x_ref.1, ...), custom_call_target="tpu_custom_call" | custom-call | tf_op jit(solution)/shard_map/pallas_call | solution.py:376
  20.2 0.0 copy-start
  20.2 1.6 %copy.20 = bf16[1,64,1024]{2,1,0:T(8,128)(2,1)} copy(bf16[1,64,1024]{2,1,0:T(8,128)(2,1)} %get-tuple-element.10) | data formatting | bytes 262144
  21.8 0.0 copy-done
  21.8 0.0 copy-start.3
  21.8 0.0 copy-start.2
  21.8 0.7 %copy.21 = bf16[1,64,1024]{2,1,0:T(8,128)(2,1)} copy(bf16[1,64,1024]{2,1,0:T(8,128)(2,1)S(1)} %copy-done) | data formatting | bytes 262144
  22.4 0.0 copy-done.3
  22.5 0.6 %copy.22 = f32[1,1024]{1,0:T(1,128)} copy(f32[1,1024]{1,0:T(1,128)S(1)} %copy-done.3) | data formatting | bytes 8192
  23.1 0.0 copy-done.2
  23.1 0.0 copy-start.1
  23.1 0.6 %copy.23 = f32[16,1024]{1,0:T(8,128)} copy(f32[16,1024]{1,0:T(8,128)S(1)} %copy-done.2) | data formatting | bytes 131072
  23.7 0.2 copy-done.1
  23.9 0.6 %copy.24 = f32[16,1024]{1,0:T(8,128)} copy(f32[16,1024]{1,0:T(8,128)S(1)} %copy-done.1) | data formatting | bytes 131072
Async XLA Ops:
  20.2 1.6 %copy-start = (bf16[1,64,1024]{2,1,0:T(8,128)(2,1)S(1)}, bf16[1,64,1024]{2,1,0:T(8,128)(2,1)}, u32[]{:S(2)}) copy-start(bf16[1,64,1024]{2,1,0:T(8,128)(2,1)} %get-tuple-element.11) | copy-start | bytes 393220
  21.8 0.7 %copy-start.3 = (f32[1,1024]{1,0:T(1,128)S(1)}, f32[1,1024]{1,0:T(1,128)}, u32[]{:S(2)}) copy-start(f32[1,1024]{1,0:T(1,128)} %get-tuple-element.12) | copy-start | bytes 12292
  21.8 1.3 %copy-start.2 = (f32[16,1024]{1,0:T(8,128)S(1)}, f32[16,1024]{1,0:T(8,128)}, u32[]{:S(2)}) copy-start(f32[16,1024]{1,0:T(8,128)} %get-tuple-element.13) | copy-start | bytes 196612
  23.1 0.9 %copy-start.1 = (f32[16,1024]{1,0:T(8,128)S(1)}, f32[16,1024]{1,0:T(8,128)}, u32[]{:S(2)}) copy-start(f32[16,1024]{1,0:T(8,128)} %get-tuple-element.14) | copy-start | bytes 196612

commit v2 on v1

v2 whole, which is shorter than its diff:
```python
import functools
import jax
import jax.numpy as jnp
from jax import lax
from jax.experimental import pallas as pl
from jax.experimental.pallas import tpu as pltpu
from jax.sharding import PartitionSpec as P

Q = 128
SCHEDULE = ((0, 2), (1, 3, 5, 6))
HIGH = lax.Precision.HIGHEST
F32 = jnp.float32
BF16 = jnp.bfloat16
MESH = pl.DeviceIdType.MESH


def mm(a, b, ca, cb):
    return lax.dot_general(a, b, (((ca,), (cb,)), ((), ())), preferred_element_type=F32)


def split(v):
    hi = v.astype(BF16)
    return hi, (v - hi.astype(F32)).astype(BF16)


def lanes(a, b):
    return jnp.concatenate([a, b], axis=1)


def rows(a, b):
    return jnp.concatenate([a, b], axis=0)


def kernel(cfg, rate_ref, skip_ref, len_ref, x_ref, dt_ref, b_ref, c_ref, g_ref, *refs):
    n_ctx, n_head, hops, fused, ndoc = cfg
    mixed_ref, gx_ref, gdt_ref, gb_ref, gc_ref = refs[:5]
    (s_ref, gz_ref, ddt_ref, out_s, out_g, in_s, in_g, ctx_send, ctx_recv) = refs[5:14]
    if fused:
        part, recv1, summed, recv2, later, recv3, sems_send, sems_recv = refs[14:]
    width_p = x_ref.shape[1]
    local = x_ref.shape[2]
    width_n = b_ref.shape[0]
    blocks = local // Q
    me = lax.axis_index("ctx")
    head = lax.axis_index("head")
    core = lax.rem(head, 2)
    at_x = lax.rem(head // 2, 2)
    at_y = head // 4
    pair_peer = head + 1 - 2 * core
    x_peer = head + 2 - 4 * at_x
    y_peer = head + 4 - 8 * at_y

    barrier = pltpu.get_barrier_semaphore()

    @pl.when(me > 0)
    def _():
        pl.semaphore_signal(barrier, inc=1, device_id={"ctx": me - 1}, device_id_type=MESH)

    @pl.when(me < n_ctx - 1)
    def _():
        pl.semaphore_signal(barrier, inc=1, device_id={"ctx": me + 1}, device_id_type=MESH)

    if fused:
        for peer in (pair_peer, x_peer, y_peer):
            pl.semaphore_signal(barrier, inc=1, device_id={"head": peer}, device_id_type=MESH)

    rate = rate_ref[0]
    skip = skip_ref[0]
    offset = me * local

    ends = []
    total = len_ref[0]
    for j in range(ndoc - 1):
        ends.append(total)
        total = total + len_ref[j + 1]

    def segment_of(pos):
        seg = jnp.zeros(pos.shape, jnp.int32)
        for end in ends:
            seg = seg + (pos >= end).astype(jnp.int32)
        return seg

    pos8 = (
        offset
        + lax.broadcasted_iota(jnp.int32, (blocks, Q), 0) * Q
        + lax.broadcasted_iota(jnp.int32, (blocks, Q), 1)
    )
    pos_t = (
        offset
        + lax.broadcasted_iota(jnp.int32, (Q, blocks), 1) * Q
        + lax.broadcasted_iota(jnp.int32, (Q, blocks), 0)
    )
    seg8 = segment_of(pos8)
    seg_t = segment_of(pos_t)
    before8 = jnp.where(pos8 == 0, -1, segment_of(pos8 - 1))
    prev8 = before8[:, 0:1]
    last8 = seg8[:, Q - 1 : Q]

    dt8 = jnp.concatenate([dt_ref[0:1, k * Q : (k + 1) * Q] for k in range(blocks)], axis=0)
    row_i = lax.broadcasted_iota(jnp.int32, (Q, Q), 0)
    col_j = lax.broadcasted_iota(jnp.int32, (Q, Q), 1)
    lower = row_i >= col_j
    lower_ones = lower.astype(F32)
    log8 = -rate * dt8
    cum8 = lax.dot_general(
        log8, lower_ones, (((1,), (1,)), ((), ())), precision=HIGH, preferred_element_type=F32
    )
    cum_t = lax.dot_general(
        lower_ones, log8, (((1,), (1,)), ((), ())), precision=HIGH, preferred_element_type=F32
    )
    end8 = cum8[:, Q - 1 : Q]
    din8 = jnp.where(seg8 == prev8, jnp.exp(cum8), 0.0)
    wdt8 = jnp.where(seg8 == last8, jnp.exp(end8 - cum8), 0.0) * dt8
    dall8 = jnp.where(last8 == prev8, jnp.exp(end8), 0.0)

    def cut(ref, k):
        return ref[0, :, k * Q : (k + 1) * Q]

    def cut2(ref, k):
        return ref[:, k * Q : (k + 1) * Q]

    state = jnp.zeros((width_p, width_n), F32)
    for k in range(blocks):
        s_ref[k] = state
        b_k = cut2(b_ref, k)
        hi, lo = split(cut(x_ref, k).astype(F32) * wdt8[k : k + 1])
        state = dall8[k : k + 1] * state + mm(lanes(hi, lo), lanes(b_k, b_k), 1, 1)
    out_s[0] = state

    def ctx_copy(r, way):
        src, dst = (out_s, in_s) if way == 0 else (out_g, in_g)
        return pltpu.make_async_remote_copy(
            src_ref=src.at[r],
            dst_ref=dst.at[r],
            send_sem=ctx_send.at[r, way],
            recv_sem=ctx_recv.at[r, way],
            device_id={"ctx": me + 1 if way == 0 else me - 1},
            device_id_type=MESH,
        )

    def ctx_start_s(r):
        @pl.when(me < n_ctx - 1)
        def _():
            ctx_copy(r, 0).start()

    def ctx_start_g(r):
        @pl.when(me > 0)
        def _():
            ctx_copy(r, 1).start()

    def ctx_wait(r):
        @pl.when(me > 0)
        def _():
            ctx_copy(r, 0).wait_recv()

        @pl.when(me < n_ctx - 1)
        def _():
            ctx_copy(r, 1).wait_recv()

    def ctx_done(r):
        @pl.when(me < n_ctx - 1)
        def _():
            ctx_copy(r, 0).wait_send()

        @pl.when(me > 0)
        def _():
            ctx_copy(r, 1).wait_send()

    @pl.when(me == 0)
    def _():
        in_s[...] = jnp.zeros_like(in_s)

    @pl.when(me == n_ctx - 1)
    def _():
        in_g[...] = jnp.zeros_like(in_g)

    peers = 3 if fused else 0
    at_end = (me == 0) | (me == n_ctx - 1)

    @pl.when(at_end)
    def _():
        pl.semaphore_wait(barrier, peers + 1)

    @pl.when(jnp.logical_not(at_end))
    def _():
        pl.semaphore_wait(barrier, peers + 2)

    ctx_start_s(0)
    carry = jnp.zeros((width_p, width_n), F32)
    for k in reversed(range(blocks)):
        gz_ref[k] = carry
        c_k = cut2(c_ref, k)
        hi, lo = split(cut(g_ref, k).astype(F32) * din8[k : k + 1])
        carry = dall8[k : k + 1] * carry + mm(lanes(hi, lo), lanes(c_k, c_k), 1, 1)
    out_g[0] = carry
    ctx_start_g(0)

    ahead = [None] * blocks
    prod = jnp.ones((1, 1), F32)
    for k in range(blocks):
        ahead[k] = prod
        prod = prod * dall8[k : k + 1]
    decay_dev = prod
    behind = [None] * blocks
    prod = jnp.ones((1, 1), F32)
    for k in reversed(range(blocks)):
        behind[k] = prod
        prod = prod * dall8[k : k + 1]

    def put(k, way, value, add):
        if fused:
            each = width_n // n_head
            chunk, lo = k // 2, (k % 2) * Q
            for h in range(n_head):
                c, x, y = h % 2, (h // 2) % 2, h // 4
                one, two = (x, y) if way == 0 else (y, x)
                at = (chunk, c, way, one, two, slice(None), slice(lo, lo + Q))
                piece = value[h * each : (h + 1) * each]
                part[at] = part[at] + piece if add else piece
        else:
            ref = (gb_ref, gc_ref)[way]
            at = (slice(None), slice(k * Q, (k + 1) * Q))
            ref[at] = ref[at] + value if add else value

    def intra_w(k):
        x_k, g_k, b_k, c_k = cut(x_ref, k), cut(g_ref, k), cut2(b_ref, k), cut2(c_ref, k)
        mask = lower & (seg_t[:, k : k + 1] == seg8[k : k + 1])
        gap = jnp.where(mask, cum_t[:, k : k + 1] - cum8[k : k + 1], 0.0)
        ddt = jnp.where(mask, jnp.exp(gap), 0.0) * dt8[k : k + 1]
        ddt_ref[k] = ddt
        w_hi, w_lo = split(mm(g_k, x_k, 0, 0) * ddt)
        put(k, 0, mm(lanes(c_k, c_k), rows(w_hi, w_lo), 1, 0), False)
        put(k, 1, mm(lanes(b_k, b_k), lanes(w_hi, w_lo), 1, 1), False)

    diffs, qs, tails = [None] * blocks, [None] * blocks, [None] * blocks

    def inter_w(k, state_in, grad_in):
        x_k, g_k = cut(x_ref, k), cut(g_ref, k)
        s_k = s_ref[k] + ahead[k] * state_in
        gz = gz_ref[k] + behind[k] * grad_in
        s_ref[k] = s_k
        gz_ref[k] = gz
        s_hi, s_lo = split(s_k)
        z_hi, z_lo = split(gz)
        put(k, 0, mm(rows(z_hi, z_lo), rows(x_k, x_k), 0, 0) * wdt8[k : k + 1], True)
        put(k, 1, mm(rows(s_hi, s_lo), rows(g_k, g_k), 0, 0) * din8[k : k + 1], True)

    def outer(k, state_in):
        x_k, g_k, b_k, c_k = cut(x_ref, k), cut(g_ref, k), cut2(b_ref, k), cut2(c_ref, k)
        s_k = s_ref[k]
        gz = gz_ref[k]
        s_end = s_ref[k + 1] if k + 1 < blocks else out_s[0] + decay_dev * state_in
        tails[k] = jnp.sum(jnp.sum(gz * s_end, axis=0, keepdims=True), axis=1, keepdims=True)
        a_hi, a_lo = split(mm(c_k, b_k, 0, 0) * ddt_ref[k])
        s_hi, s_lo = split(s_k)
        z_hi, z_lo = split(gz)
        din, wdt = din8[k : k + 1], wdt8[k : k + 1]
        y = mm(lanes(x_k, x_k), lanes(a_hi, a_lo), 1, 1)
        y = y + mm(lanes(s_hi, s_lo), rows(c_k, c_k), 1, 0) * din
        v = mm(lanes(g_k, g_k), rows(a_hi, a_lo), 1, 0)
        v = v + mm(lanes(z_hi, z_lo), rows(b_k, b_k), 1, 0) * wdt
        x_f, g_f = x_k.astype(F32), g_k.astype(F32)
        mixed_ref[0, :, k * Q : (k + 1) * Q] = (y + skip * x_f).astype(BF16)
        gx_ref[0, :, k * Q : (k + 1) * Q] = (v + skip * g_f).astype(BF16)
        q_k = jnp.sum(x_f * v, axis=0, keepdims=True)
        qs[k] = q_k
        diffs[k] = jnp.sum(g_f * y, axis=0, keepdims=True) - q_k

    coord = (at_x, at_y)
    peer_of = (x_peer, y_peer)

    def hop(src, dst, chunk, stage, to):
        return pltpu.make_async_remote_copy(
            src_ref=src,
            dst_ref=dst,
            send_sem=sems_send.at[chunk, stage],
            recv_sem=sems_recv.at[chunk, stage],
            device_id={"head": to},
            device_id_type=MESH,
        )

    def pair_copy(chunk):
        return hop(part.at[chunk, 1 - core], recv1.at[chunk], chunk, 0, pair_peer)

    def first_copy(chunk, way):
        src = summed.at[chunk, way, 1 - coord[way]]
        return hop(src, recv2.at[chunk, way], chunk, 1 + way, peer_of[way])

    def second_copy(chunk, way):
        src = later.at[chunk, way, 1 - coord[1 - way]]
        return hop(src, recv3.at[chunk, way], chunk, 3 + way, peer_of[1 - way])

    def first(chunk):
        pair_copy(chunk).wait_recv()
        summed[chunk] = part[chunk, core] + recv1[chunk]
        for way in range(2):
            first_copy(chunk, way).start()

    def second(chunk):
        for way in range(2):
            first_copy(chunk, way).wait_recv()
            later[chunk, way] = summed[chunk, way, coord[way]] + recv2[chunk, way]
            second_copy(chunk, way).start()

    for k in range(blocks):
        intra_w(k)
    ctx_wait(0)
    for r in range(1, hops):
        out_s[r] = out_s[0] + decay_dev * in_s[r - 1]
        out_g[r] = out_g[0] + decay_dev * in_g[r - 1]
        ctx_start_s(r)
        ctx_start_g(r)
        ctx_wait(r)
    state_in = in_s[hops - 1]
    grad_in = in_g[hops - 1]
    for k in range(blocks):
        inter_w(k, state_in, grad_in)
        if fused and k % 2 == 1:
            pair_copy(k // 2).start()
            if k >= 5:
                first(k // 2 - 2)
    chunks = blocks // 2
    firsts, seconds = SCHEDULE
    for k in range(blocks):
        if fused:
            for chunk in range(chunks):
                if chunk >= chunks - 2 and firsts[chunk - chunks + 2] == k:
                    first(chunk)
                if seconds[chunk] == k:
                    second(chunk)
        outer(k, state_in)

    q8 = jnp.concatenate(qs, axis=0)
    r8 = jnp.concatenate(diffs, axis=0)
    tail8 = jnp.concatenate(tails, axis=0)
    back8 = lax.dot_general(
        r8, lower_ones, (((1,), (0,)), ((), ())), precision=HIGH, preferred_element_type=F32
    )
    gdt8 = q8 / dt8 - rate * (back8 + tail8)
    for k in range(blocks):
        gdt_ref[0:1, k * Q : (k + 1) * Q] = gdt8[k : k + 1]

    for r in range(hops):
        ctx_done(r)
    if fused:
        for chunk in range(chunks):
            at = slice(chunk * 2 * Q, (chunk + 1) * 2 * Q)
            for way in range(2):
                second_copy(chunk, way).wait_recv()
                own = later[chunk, way, coord[1 - way]]
                (gb_ref, gc_ref)[way][:, at] = own + recv3[chunk, way]
        for chunk in range(chunks):
            pair_copy(chunk).wait_send()
            for way in range(2):
                first_copy(chunk, way).wait_send()
                second_copy(chunk, way).wait_send()


def move(*refs):
    count = len(refs) // 2
    for i in range(count):
        refs[count + i][...] = refs[i][...]


def per_device(n_ctx, n_head, inputs, dt, decay_rate, skip, b_proj, c_proj, lengths, grad_out):
    _, width_p, local = inputs.shape
    width_n = b_proj.shape[0]
    longest = n_ctx * local // 4
    hops = max(1, min(n_ctx - 1, (longest - 2) // local + 1))
    each = width_n // n_head
    fused = n_head == 8 and each % 8 == 0 and local == 8 * Q
    blocks = local // Q
    chunks = blocks // 2
    vmem = pl.BlockSpec(memory_space=pltpu.VMEM)
    smem = pl.BlockSpec(memory_space=pltpu.SMEM)
    grad_rows = each if fused else width_n
    scratch = [
        pltpu.VMEM((blocks, width_p, width_n), F32),
        pltpu.VMEM((blocks, width_p, width_n), F32),
        pltpu.VMEM((blocks, Q, Q), F32),
        pltpu.VMEM((hops, width_p, width_n), F32),
        pltpu.VMEM((hops, width_p, width_n), F32),
        pltpu.VMEM((hops, width_p, width_n), F32),
        pltpu.VMEM((hops, width_p, width_n), F32),
        pltpu.SemaphoreType.DMA((hops, 2)),
        pltpu.SemaphoreType.DMA((hops, 2)),
    ]
    if fused:
        scratch += [
            pltpu.VMEM((chunks, 2, 2, 2, 2, each, 2 * Q), F32),
            pltpu.VMEM((chunks, 2, 2, 2, each, 2 * Q), F32),
            pltpu.VMEM((chunks, 2, 2, 2, each, 2 * Q), F32),
            pltpu.VMEM((chunks, 2, 2, each, 2 * Q), F32),
            pltpu.VMEM((chunks, 2, 2, each, 2 * Q), F32),
            pltpu.VMEM((chunks, 2, each, 2 * Q), F32),
            pltpu.SemaphoreType.DMA((chunks, 5)),
            pltpu.SemaphoreType.DMA((chunks, 5)),
        ]
    mixed, gx, gdt, gb, gc = pl.pallas_call(
        functools.partial(kernel, (n_ctx, n_head, hops, fused, lengths.shape[0])),
        out_shape=(
            jax.ShapeDtypeStruct(inputs.shape, BF16),
            jax.ShapeDtypeStruct(inputs.shape, BF16),
            jax.ShapeDtypeStruct(dt.shape, F32),
            jax.ShapeDtypeStruct((grad_rows, local), F32),
            jax.ShapeDtypeStruct((grad_rows, local), F32),
        ),
        in_specs=[smem, smem, smem, vmem, vmem, vmem, vmem, vmem],
        out_specs=(vmem,) * 5,
        scratch_shapes=scratch,
        compiler_params=pltpu.CompilerParams(collective_id=0, has_side_effects=True),
    )(decay_rate, skip, lengths, inputs, dt, b_proj, c_proj, grad_out)
    if not fused:
        gb = lax.psum_scatter(gb, "head", scatter_dimension=0, tiled=True)
        gc = lax.psum_scatter(gc, "head", scatter_dimension=0, tiled=True)
    results = (mixed, gx, gdt, gb, gc)
    hbm = pl.BlockSpec(memory_space=pltpu.VMEM)
    return pl.pallas_call(
        move,
        out_shape=tuple(jax.ShapeDtypeStruct(r.shape, r.dtype) for r in results),
        in_specs=[hbm] * 5,
        out_specs=(hbm,) * 5,
    )(*results)


def solution(mesh):
    return jax.shard_map(
        functools.partial(per_device, mesh.shape["ctx"], mesh.shape["head"]),
        mesh=mesh,
        in_specs=(
            P("head", None, "ctx"),
            P("head", "ctx"),
            P("head"),
            P("head"),
            P(None, "ctx"),
            P(None, "ctx"),
            P(),
            P("head", None, "ctx"),
        ),
        out_specs=(
            P("head", None, "ctx"),
            P("head", None, "ctx"),
            P("head", "ctx"),
            P("head", "ctx"),
            P("head", "ctx"),
        ),
        check_vma=False,
    )
```

time: 24.8 us -> 23.7 us (0.956)
  local copies, waits for them, and re-layouts: 4.37 us -> 0 us
  Pallas kernels: 18.2 us -> 21.6 us
    unnamed x13 -> x0, local copies, waits for them, and re-layouts: 4.37 us -> none
    pallas_call x0 -> x1, Pallas kernels: none -> 1.76 us  [per_device(): pl.pallas_call(move, out_shape=tuple((jax.ShapeDtypeStruct(r.shape, r.dty...]
    pallas_call x1, Pallas kernels: 18.2 us -> 19.8 us  [per_device(): pl.pallas_call(functools.partial(kernel, (n_ctx, n_head, hops, fused, len...]
where the time goes in v2:
time: 23.7 us; the launch traced here: 23.5 us
  Pallas kernels  21.6 us (91%)
  between operations  1.93 us (8%)
    pallas_call x1, Pallas kernels, per_device(): pl.pallas_call(functools.partial(kernel, (n_ctx, n_head, hops, fused, len...  19.8 us
    pallas_call x1, Pallas kernels, per_device(): pl.pallas_call(move, out_shape=tuple((jax.ShapeDtypeStruct(r.shape, r.dty...  1.76 us

profile of v2, /device:TPU:0, one launch (start us, length us, event | category | flops | bytes accessed | tf_op | source)
XLA Modules:
  0.0 23.5 jit_solution(14896855448789770775)
XLA Ops:
  1.9 19.8 %shard_map.119 = (bf16[1,64,1024]{2,1,0:T(8,128)(2,1)}, bf16[1,64,1024]{2,1,0:T(8,128)(2,1)}, f32[1,1024]{1,0:T(1,128)}, f32[16,1024]{1,0:T(8,128)}, f32[16,1024]{1,0:T(8,128)}) custom-call(f32[1]{0:T(128)S(6)} %copy.13.rate_ref, f32[1]{0:T(128)S(6)} %copy.14.skip_ref, s32[16]{0:T(128)} %len_ref.1, bf16[1,64,1024]{2,1,0:T(8,128)(2,1)} %x_ref.1, ...), custom_call_target="tpu_custom_call" | custom-call | tf_op jit(solution)/shard_map/pallas_call | solution.py:399
  21.8 1.8 %shard_map.120 = (bf16[1,64,1024]{2,1,0:T(8,128)(2,1)}, bf16[1,64,1024]{2,1,0:T(8,128)(2,1)}, f32[1,1024]{1,0:T(1,128)}, f32[16,1024]{1,0:T(8,128)}, f32[16,1024]{1,0:T(8,128)}) custom-call(bf16[1,64,1024]{2,1,0:T(8,128)(2,1)} %get-tuple-element.10.refs_0_, bf16[1,64,1024]{2,1,0:T(8,128)(2,1)} %get-tuple-element.11.refs_1_, ...), custom_call_target="tpu_custom_call" | custom-call | tf_op jit(solution)/shard_map/pallas_call | solution.py:418

commit v3 on v1

--- a/solution.py
+++ b/solution.py
@@ -33,9 +33,9 @@
 def kernel(cfg, rate_ref, skip_ref, len_ref, x_ref, dt_ref, b_ref, c_ref, g_ref, *refs):
     n_ctx, n_head, hops, fused, ndoc = cfg
     mixed_ref, gx_ref, gdt_ref, gb_ref, gc_ref = refs[:5]
-    (s_ref, gz_ref, y_ref, v_ref, out_s, out_g, in_s, in_g, ctx_send, ctx_recv) = refs[5:15]
+    (s_ref, gz_ref, ddt_ref, out_s, out_g, in_s, in_g, ctx_send, ctx_recv) = refs[5:14]
     if fused:
-        part, recv1, send2, recv2, s1_send, s1_recv, s2_send, s2_recv = refs[15:]
+        part, recv1, send2, recv2, s1_send, s1_recv, s2_send, s2_recv = refs[14:]
     width_p = x_ref.shape[1]
     local = x_ref.shape[2]
     width_n = b_ref.shape[0]
@@ -218,46 +218,49 @@
             at = (slice(None), slice(k * Q, (k + 1) * Q))
             ref[at] = ref[at] + value if add else value
 
-    def intra(k):
+    def intra_w(k):
         x_k, g_k, b_k, c_k = cut(x_ref, k), cut(g_ref, k), cut2(b_ref, k), cut2(c_ref, k)
         mask = lower & (seg_t[:, k : k + 1] == seg8[k : k + 1])
         gap = jnp.where(mask, cum_t[:, k : k + 1] - cum8[k : k + 1], 0.0)
         ddt = jnp.where(mask, jnp.exp(gap), 0.0) * dt8[k : k + 1]
-        a_hi, a_lo = split(mm(c_k, b_k, 0, 0) * ddt)
+        ddt_ref[k] = ddt
         w_hi, w_lo = split(mm(g_k, x_k, 0, 0) * ddt)
-        y_ref[:, k * Q : (k + 1) * Q] = mm(lanes(x_k, x_k), lanes(a_hi, a_lo), 1, 1)
-        v_ref[:, k * Q : (k + 1) * Q] = mm(lanes(g_k, g_k), rows(a_hi, a_lo), 1, 0)
         put(k, 0, mm(lanes(c_k, c_k), rows(w_hi, w_lo), 1, 0), False)
         put(k, 1, mm(lanes(b_k, b_k), lanes(w_hi, w_lo), 1, 1), False)
 
     diffs, qs, tails = [None] * blocks, [None] * blocks, [None] * blocks
 
-    def start_state(k, state_in):
-        return s_ref[k] + ahead[k] * state_in
-
-    def inter(k, state_in, grad_in):
+    def inter_w(k, state_in, grad_in):
+        x_k, g_k = cut(x_ref, k), cut(g_ref, k)
+        s_k = s_ref[k] + ahead[k] * state_in
+        gz = gz_ref[k] + behind[k] * grad_in
+        s_ref[k] = s_k
+        gz_ref[k] = gz
+        s_hi, s_lo = split(s_k)
+        z_hi, z_lo = split(gz)
+        put(k, 0, mm(rows(z_hi, z_lo), rows(x_k, x_k), 0, 0) * wdt8[k : k + 1], True)
+        put(k, 1, mm(rows(s_hi, s_lo), rows(g_k, g_k), 0, 0) * din8[k : k + 1], True)
+
+    def outer(k, state_in):
         x_k, g_k, b_k, c_k = cut(x_ref, k), cut(g_ref, k), cut2(b_ref, k), cut2(c_ref, k)
-        s_k = start_state(k, state_in)
-        gz = gz_ref[k] + behind[k] * grad_in
-        if k + 1 < blocks:
-            s_end = start_state(k + 1, state_in)
-        else:
-            s_end = out_s[0] + decay_dev * state_in
+        s_k = s_ref[k]
+        gz = gz_ref[k]
+        s_end = s_ref[k + 1] if k + 1 < blocks else out_s[0] + decay_dev * state_in
         tails[k] = jnp.sum(jnp.sum(gz * s_end, axis=0, keepdims=True), axis=1, keepdims=True)
+        a_hi, a_lo = split(mm(c_k, b_k, 0, 0) * ddt_ref[k])
         s_hi, s_lo = split(s_k)
         z_hi, z_lo = split(gz)
         din, wdt = din8[k : k + 1], wdt8[k : k + 1]
-        at = (slice(None), slice(k * Q, (k + 1) * Q))
-        y = y_ref[at] + mm(lanes(s_hi, s_lo), rows(c_k, c_k), 1, 0) * din
-        v = v_ref[at] + mm(lanes(z_hi, z_lo), rows(b_k, b_k), 1, 0) * wdt
+        y = mm(lanes(x_k, x_k), lanes(a_hi, a_lo), 1, 1)
+        y = y + mm(lanes(s_hi, s_lo), rows(c_k, c_k), 1, 0) * din
+        v = mm(lanes(g_k, g_k), rows(a_hi, a_lo), 1, 0)
+        v = v + mm(lanes(z_hi, z_lo), rows(b_k, b_k), 1, 0) * wdt
         x_f, g_f = x_k.astype(F32), g_k.astype(F32)
         mixed_ref[0, :, k * Q : (k + 1) * Q] = (y + skip * x_f).astype(BF16)
         gx_ref[0, :, k * Q : (k + 1) * Q] = (v + skip * g_f).astype(BF16)
         q_k = jnp.sum(x_f * v, axis=0, keepdims=True)
         qs[k] = q_k
         diffs[k] = jnp.sum(g_f * y, axis=0, keepdims=True) - q_k
-        put(k, 0, mm(rows(z_hi, z_lo), rows(x_k, x_k), 0, 0) * wdt, True)
-        put(k, 1, mm(rows(s_hi, s_lo), rows(g_k, g_k), 0, 0) * din, True)
 
     def pair_copy(chunk):
         return pltpu.make_async_remote_copy(
@@ -286,9 +289,8 @@
         for d in range(1, chips):
             chip_copy(chunk, d).start()
 
-    early = blocks // 2
-    for k in range(early):
-        intra(k)
+    for k in range(blocks):
+        intra_w(k)
     ctx_wait(0)
     for r in range(1, hops):
         out_s[r] = out_s[0] + decay_dev * in_s[r - 1]
@@ -298,14 +300,13 @@
     state_in = in_s[hops - 1]
     grad_in = in_g[hops - 1]
     for k in range(blocks):
-        if k >= early:
-            intra(k)
-        inter(k, state_in, grad_in)
+        inter_w(k, state_in, grad_in)
         if fused and k % 2 == 1:
-            chunk = k // 2
-            pair_copy(chunk).start()
-            if chunk > 0:
-                second(chunk - 1)
+            pair_copy(k // 2).start()
+    for k in range(blocks):
+        if fused and k < blocks // 2:
+            second(k)
+        outer(k, state_in)
 
     q8 = jnp.concatenate(qs, axis=0)
     r8 = jnp.concatenate(diffs, axis=0)
@@ -322,7 +323,6 @@
     if fused:
         each = width_n // n_head
         chunks = blocks // 2
-        second(chunks - 1)
         for chunk in range(chunks):
             total = send2[chunk, chip]
             for d in range(1, chips):
@@ -335,6 +335,12 @@
             pair_copy(chunk).wait_send()
             for d in range(1, chips):
                 chip_copy(chunk, d).wait_send()
+
+
+def move(*refs):
+    count = len(refs) // 2
+    for i in range(count):
+        refs[count + i][...] = refs[i][...]
 
 
 def per_device(n_ctx, n_head, inputs, dt, decay_rate, skip, b_proj, c_proj, lengths, grad_out):
@@ -353,8 +359,7 @@
     scratch = [
         pltpu.VMEM((blocks, width_p, width_n), F32),
         pltpu.VMEM((blocks, width_p, width_n), F32),
-        pltpu.VMEM((width_p, local), F32),
-        pltpu.VMEM((width_p, local), F32),
+        pltpu.VMEM((blocks, Q, Q), F32),
         pltpu.VMEM((hops, width_p, width_n), F32),
         pltpu.VMEM((hops, width_p, width_n), F32),
         pltpu.VMEM((hops, width_p, width_n), F32),
@@ -390,7 +395,14 @@
     if not fused:
         gb = lax.psum_scatter(gb, "head", scatter_dimension=0, tiled=True)
         gc = lax.psum_scatter(gc, "head", scatter_dimension=0, tiled=True)
-    return mixed, gx, gdt, gb, gc
+    results = (mixed, gx, gdt, gb, gc)
+    hbm = pl.BlockSpec(memory_space=pltpu.VMEM)
+    return pl.pallas_call(
+        move,
+        out_shape=tuple(jax.ShapeDtypeStruct(r.shape, r.dtype) for r in results),
+        in_specs=[hbm] * 5,
+        out_specs=(hbm,) * 5,
+    )(*results)
 
 
 def solution(mesh):

time: 24.8 us -> 22.5 us (0.907)
  local copies, waits for them, and re-layouts: 4.37 us -> 0 us
  Pallas kernels: 18.2 us -> 20.4 us
    unnamed x13 -> x0, local copies, waits for them, and re-layouts: 4.37 us -> none
    pallas_call x0 -> x1, Pallas kernels: none -> 1.76 us  [per_device(): pl.pallas_call(move, out_shape=tuple((jax.ShapeDtypeStruct(r.shape, r.dty...]
    pallas_call x1, Pallas kernels: 18.2 us -> 18.7 us  [per_device(): pl.pallas_call(functools.partial(kernel, (n_ctx, n_head, hops, fused, len...]
where the time goes in v3:
time: 22.5 us; the launch traced here: 22.4 us
  Pallas kernels  20.4 us (91%)
  between operations  1.93 us (9%)
    pallas_call x1, Pallas kernels, per_device(): pl.pallas_call(functools.partial(kernel, (n_ctx, n_head, hops, fused, len...  18.7 us
    pallas_call x1, Pallas kernels, per_device(): pl.pallas_call(move, out_shape=tuple((jax.ShapeDtypeStruct(r.shape, r.dty...  1.76 us

profile of v3, /device:TPU:0, one launch (start us, length us, event | category | flops | bytes accessed | tf_op | source)
XLA Modules:
  0.0 22.4 jit_solution(8789475345374933395)
XLA Ops:
  1.9 18.7 %shard_map.119 = (bf16[1,64,1024]{2,1,0:T(8,128)(2,1)}, bf16[1,64,1024]{2,1,0:T(8,128)(2,1)}, f32[1,1024]{1,0:T(1,128)}, f32[16,1024]{1,0:T(8,128)}, f32[16,1024]{1,0:T(8,128)}) custom-call(f32[1]{0:T(128)S(6)} %copy.13.rate_ref, f32[1]{0:T(128)S(6)} %copy.14.skip_ref, s32[16]{0:T(128)} %len_ref.1, bf16[1,64,1024]{2,1,0:T(8,128)(2,1)} %x_ref.1, ...), custom_call_target="tpu_custom_call" | custom-call | tf_op jit(solution)/shard_map/pallas_call | solution.py:381
  20.6 1.8 %shard_map.120 = (bf16[1,64,1024]{2,1,0:T(8,128)(2,1)}, bf16[1,64,1024]{2,1,0:T(8,128)(2,1)}, f32[1,1024]{1,0:T(1,128)}, f32[16,1024]{1,0:T(8,128)}, f32[16,1024]{1,0:T(8,128)}) custom-call(bf16[1,64,1024]{2,1,0:T(8,128)(2,1)} %get-tuple-element.10.refs_0_, bf16[1,64,1024]{2,1,0:T(8,128)(2,1)} %get-tuple-element.11.refs_1_, ...), custom_call_target="tpu_custom_call" | custom-call | tf_op jit(solution)/shard_map/pallas_call | solution.py:400

commit v4 on v3

--- a/solution.py
+++ b/solution.py
@@ -286,7 +286,7 @@
     def second(chunk):
         pair_copy(chunk).wait_recv()
         send2[chunk] = part[chunk, core] + recv1[chunk]
-        for d in range(1, chips):
+        for d in list(range(1, chips, 2)) + list(range(2, chips, 2)):
             chip_copy(chunk, d).start()
 
     for k in range(blocks):

time: 22.5 us -> 22.5 us (level)
  no operation moved by 1% of the time
where the time goes in v4:
time: 22.5 us; the launch traced here: 22.4 us
  Pallas kernels  20.4 us (91%)
  between operations  1.93 us (9%)
    pallas_call x1, Pallas kernels, per_device(): pl.pallas_call(functools.partial(kernel, (n_ctx, n_head, hops, fused, len...  18.7 us
    pallas_call x1, Pallas kernels, per_device(): pl.pallas_call(move, out_shape=tuple((jax.ShapeDtypeStruct(r.shape, r.dty...  1.76 us

profile of v4, /device:TPU:0, one launch (start us, length us, event | category | flops | bytes accessed | tf_op | source)
XLA Modules:
  0.0 22.4 jit_solution(11683957171487355999)
XLA Ops:
  1.9 18.7 %shard_map.119 = (bf16[1,64,1024]{2,1,0:T(8,128)(2,1)}, bf16[1,64,1024]{2,1,0:T(8,128)(2,1)}, f32[1,1024]{1,0:T(1,128)}, f32[16,1024]{1,0:T(8,128)}, f32[16,1024]{1,0:T(8,128)}) custom-call(f32[1]{0:T(128)S(6)} %copy.13.rate_ref, f32[1]{0:T(128)S(6)} %copy.14.skip_ref, s32[16]{0:T(128)} %len_ref.1, bf16[1,64,1024]{2,1,0:T(8,128)(2,1)} %x_ref.1, ...), custom_call_target="tpu_custom_call" | custom-call | tf_op jit(solution)/shard_map/pallas_call | solution.py:381
  20.6 1.8 %shard_map.120 = (bf16[1,64,1024]{2,1,0:T(8,128)(2,1)}, bf16[1,64,1024]{2,1,0:T(8,128)(2,1)}, f32[1,1024]{1,0:T(1,128)}, f32[16,1024]{1,0:T(8,128)}, f32[16,1024]{1,0:T(8,128)}) custom-call(bf16[1,64,1024]{2,1,0:T(8,128)(2,1)} %get-tuple-element.10.refs_0_, bf16[1,64,1024]{2,1,0:T(8,128)(2,1)} %get-tuple-element.11.refs_1_, ...), custom_call_target="tpu_custom_call" | custom-call | tf_op jit(solution)/shard_map/pallas_call | solution.py:400
